TPU v7x, 512 devices: a whole 4x4x16 slice. The times are simulated.
512 devices in a mesh: shell: 128 (over x, z, core), aux: 4 (over y).
Axes of the slice: x: 4, y: 4, z: 16, core: 2. Of those that a mesh axis runs over, the one named last changes fastest.
Arguments:
- integrals: bfloat16 [512, 128, 4, 128], P('shell', None, 'aux'), may hold values from -6 to 6
- pair_list: int32 [512, 3], P('shell'), may hold values from 0 to 511, as said below
- coef: bfloat16 [65536, 1024], P('shell'), may hold values from -0.5 to 0.5
- metric: bfloat16 [4, 4], replicated, may hold values from -3 to 3, as said below
- occ_slot: int32 [128], replicated, may hold values from 0 to 127, each once
Outputs:
- transformed: bfloat16 [1024, 4, 65536], P(('shell', 'aux'))
Inputs may be any that keep to these rules, and one draw needn't show every extreme that they name: `pair_list`: row d * 4 + k holds slot k of index d of shell: block row, block column, live flag. The block column lies in d * 4 to (d + 1) * 4 - 1. On every index live slots come first and at least one is live; some index has all 4 live. `metric`: lower triangular, positive on the diagonal.
All inputs are finite; a program needn't handle non-finite values.
Results may differ from a plain program's by a relative error of at most 0.0054.
Values may be sent and summed in bfloat16 or wider, within the bound.
A program may use at most 64 MiB of HBM per device.

v0:
```python
import jax
import jax.numpy as jnp
from jax import lax
from jax.sharding import PartitionSpec as P

BS = 128


def per_device(integrals, pair_list, coef, metric, occ_slot):
    pairs_dev = pair_list.shape[0]
    rows_local = coef.shape[0]
    occ_count = coef.shape[1]
    blocks_dev = rows_local // BS
    shell_count = lax.axis_size("shell")
    block_count = blocks_dev * shell_count
    slot_count = occ_slot.shape[0]
    aux_dev = integrals.shape[2]
    inverse = (
        jnp.zeros((slot_count,), jnp.int32)
        .at[occ_slot]
        .set(jnp.arange(slot_count, dtype=jnp.int32))
    )
    ordered = jnp.take(
        coef.reshape(rows_local, slot_count, occ_count // slot_count), inverse, axis=1
    )
    ordered = ordered.reshape(rows_local, occ_count)

    def one_slot(item):
        int_block, column_index = item
        start = column_index % blocks_dev * BS
        column = lax.dynamic_slice_in_dim(ordered, start, BS, 0)
        product = lax.dot_general(
            column,
            int_block.reshape(BS, aux_dev * BS),
            (((0,), (0,)), ((), ())),
            preferred_element_type=jnp.float32,
        )
        return product.astype(jnp.bfloat16)

    half_blocks = lax.map(one_slot, (integrals, pair_list[:, 1]))
    half_blocks = half_blocks.reshape(pairs_dev, occ_count, aux_dev, BS)
    listing = lax.all_gather(pair_list, "shell", axis=0, tiled=True)
    targets = jnp.arange(block_count, dtype=jnp.int32)[:, None]
    selector = ((listing[:, 0][None, :] == targets) & (listing[:, 2][None, :] == 1)).astype(
        jnp.bfloat16
    )
    relayed = lax.all_to_all(
        lax.all_to_all(half_blocks, "shell", split_axis=1, concat_axis=0, tiled=True),
        "aux",
        split_axis=1,
        concat_axis=2,
        tiled=True,
    )
    summed = jnp.dot(
        selector, relayed.reshape(relayed.shape[0], -1), preferred_element_type=jnp.float32
    )
    blocks = summed.astype(jnp.bfloat16).reshape((block_count,) + relayed.shape[1:])
    result = jnp.einsum("qp,bipm->iqbm", metric, blocks, preferred_element_type=jnp.float32)
    return result.reshape(result.shape[0], result.shape[1], block_count * BS).astype(jnp.bfloat16)


def solution(mesh):
    placed = (P("shell", None, "aux", None), P("shell", None), P("shell", None), P(), P())
    return jax.shard_map(
        per_device,
        mesh=mesh,
        in_specs=placed,
        out_specs=P(("shell", "aux"), None, None),
        check_vma=False,
    )
```

profile of v0, /device:TPU:1, one launch (start us, length us, event | category | flops | bytes accessed | tf_op | source)
XLA Modules:
  0.0 205.9 jit_solution(11804954031086884912)
XLA Ops:
  0.0 0.7 compare_select_fusion.1
  0.7 1.0 scatter_custom_fusion
  1.7 1.5 copy.23
  3.2 0.1 broadcast_in_dim.32
  3.3 0.1 broadcast_in_dim.33
  3.4 0.2 slice_reduce_fusion
  3.6 0.6 gather_fusion
  4.3 0.2 bitcast_select_fusion
  4.5 15.1 %while.12 = (s32[]{:T(128)}, bf16[4,1024,128]{2,1,0:T(8,128)(2,1)S(1)}, s32[4]{0:T(128)S(1)}, bf16[512,1024]{0,1:T(8,128)(2,1)S(1)}, bf16[4,128,1,128]{3,1,2,0:T...) while((s32[]{:T(128)}, ...), condition=%wide.region_2.3_spmd, body=%wide.region_1.2_spmd.sunk | while | flops 33685520 | bytes 558360 | solution.py:40
  4.5 0.7 dynamic_slice.31
  7.2 1.0 fusion.22
  8.3 0.7 dynamic_slice.31
  11.0 1.0 fusion.22
  12.0 0.7 dynamic_slice.31
  14.8 1.0 fusion.22
  15.8 0.7 dynamic_slice.31
  18.6 1.0 fusion.22
  19.6 0.8 copy.41
  20.4 74.5 %all_to_all.33 = bf16[4,1024,1,128]{3,0,2,1:T(4,128)(2,1)S(1)} all-to-all(bf16[4,1024,1,128]{3,0,2,1:T(4,128)(2,1)S(1)} %bitcast.50), channel_id=1, replica_groups=mesh['shell'=128,'aux'=4] {'shell'}, dimensions={1} | all-to-all | bytes 2097152 | tf_op jit(solution)/shard_map/all_to_all | solution.py:48
  94.9 0.1 copy.40
  95.1 0.2 copy.27
  95.3 1.1 copy.28
  96.4 4.2 %all-to-all-start.1 = ((bf16[512,8,1,128]{3,0,2,1:T(8,128)(2,1)}), bf16[512,8,1,128]{3,0,2,1:T(8,128)(2,1)S(1)}, u32[]{:S(2)}, u32[]{:S(2)}) async-start(bf16[512,8,1,128]{3,0,2,1:T(8,128)(2,1)} %copy.28), calls=%async_computation.1 | async-start | bytes 2097152 | tf_op jit(solution)/shard_map/all_to_all | solution.py:47
  100.6 100.8 %all-gather = s32[128,4,3]{2,1,0:T(4,128)S(1)} all-gather(s32[1,4,3]{2,1,0:T(4,128)S(1)} %bitcast.55), channel_id=1, replica_groups=mesh['shell'=128,'aux'=4] {'shell'}, dimensions={0}, use_global_device_ids=true | all-gather | bytes 6192 | tf_op jit(solution)/shard_map/all_gather | solution.py:42
  201.4 0.1 fusion.14
  201.5 0.1 copy.34
  201.7 0.1 copy.33
  201.8 0.5 copy.29
  202.4 0.7 convolution_convert_fusion.2
  203.1 0.8 reshape.43
  203.9 0.7 fusion.6
  204.6 1.3 copy.39
  (11 shorter events, 0.1 us)
Async XLA Ops:
  0.0 203.9 %copy-start = (bf16[4,4]{1,0:T(4,128)(2,1)S(1)}, bf16[4,4]{1,0:T(4,128)(2,1)}, u32[]{:S(2)}) copy-start(bf16[4,4]{1,0:T(4,128)(2,1)} %param.10) | copy-start | bytes 100
  1.7 1.7 copy-start.1
  96.4 105.4 %all-to-all-start.1 = ((bf16[512,8,1,128]{3,0,2,1:T(8,128)(2,1)}), bf16[512,8,1,128]{3,0,2,1:T(8,128)(2,1)S(1)}, u32[]{:S(2)}, u32[]{:S(2)}) async-start(bf16[512,8,1,128]{3,0,2,1:T(8,128)(2,1)} %copy.28), calls=%async_computation.1 | async-start | bytes 2097152 | tf_op jit(solution)/shard_map/all_to_all | solution.py:47
where the time goes:
time: 207 us; the launch traced here: 206 us
  blocking collectives  175 us (85%)
  local copies, waits for them, and re-layouts  11.4 us (6%)
  loops' own time  8.45 us (4%)
  matrix products  5.41 us (3%)
  starting transfers between devices  4.18 us (2%)
    all_gather x1, blocking collectives, per_device(): listing = lax.all_gather(pair_list, 'shell', axis=0, tiled=True)  101 us
    all_to_all x1, blocking collectives, per_device(): lax.all_to_all(half_blocks, 'shell', split_axis=1, concat_axis=0, tiled=T...  74.5 us
    another operation x1, loops' own time, per_device(): half_blocks = lax.map(one_slot, (integrals, pair_list[:, 1]))  8.45 us
    all_to_all x1, starting transfers between devices, per_device(): lax.all_to_all(lax.all_to_all(half_blocks, 'shell', split_axis=1, concat_...  4.18 us
  transfers between devices with their start and end apart: 1, of which 0 were waited for; matrix products, arithmetic and copies ran while one was open for 0% of the time, Pallas kernels for 0%

commit v1 on v0

--- a/solution.py
+++ b/solution.py
@@ -39,7 +39,9 @@
 
     half_blocks = lax.map(one_slot, (integrals, pair_list[:, 1]))
     half_blocks = half_blocks.reshape(pairs_dev, occ_count, aux_dev, BS)
-    listing = lax.all_gather(pair_list, "shell", axis=0, tiled=True)
+    listing = jnp.concatenate(
+        lax.all_to_all(jnp.stack([pair_list] * lax.axis_size("shell")), "shell", 0, 0), axis=0
+    )
     targets = jnp.arange(block_count, dtype=jnp.int32)[:, None]
     selector = ((listing[:, 0][None, :] == targets) & (listing[:, 2][None, :] == 1)).astype(
         jnp.bfloat16

time: 207 us -> 150 us (0.72)
  blocking collectives: 175 us -> 0 us
  waiting for transfers between devices: 0.01 us -> 87.5 us
  starting transfers between devices: 4.18 us -> 33.1 us
    all_gather x1 -> x0, blocking collectives: 101 us -> none  [per_device(): listing = lax.all_gather(pair_list, 'shell', axis=0, tiled=True)]
    all_to_all x0 -> x2, waiting for transfers between devices: none -> 75.3 us  [the longest x1 54.3 us: per_device(): lax.all_to_all(half_blocks, 'shell', split_axis=1, concat_axis=0, tiled=T...]
    all_to_all x1 -> x0, blocking collectives: 74.5 us -> none  [per_device(): lax.all_to_all(half_blocks, 'shell', split_axis=1, concat_axis=0, tiled=T...]
    all_to_all x0 -> x2, starting transfers between devices: none -> 28.9 us  [the longest x1 20.4 us: per_device(): lax.all_to_all(half_blocks, 'shell', split_axis=1, concat_axis=0, tiled=T...]
    all_to_all x1, waiting for transfers between devices: 0.01 us -> 12.2 us  [per_device(): lax.all_to_all(lax.all_to_all(half_blocks, 'shell', split_axis=1, concat_...]
  transfers between devices with their start and end apart: 1 -> 3, of which waited for: 0 -> 3; matrix products, arithmetic and copies ran while one was open for 0% -> 1% of each run, Pallas kernels for 0% -> 0%
where the time goes in v1:
time: 150 us; the launch traced here: 148 us
  waiting for transfers between devices  87.5 us (58%)
  starting transfers between devices  33.1 us (22%)
  local copies, waits for them, and re-layouts  12.8 us (9%)
  loops' own time  7.78 us (5%)
  matrix products  5.42 us (4%)
    all_to_all x1, waiting for transfers between devices, per_device(): lax.all_to_all(half_blocks, 'shell', split_axis=1, concat_axis=0, tiled=T...  54.3 us
    all_to_all x1, waiting for transfers between devices, per_device(): lax.all_to_all(jnp.stack([pair_list] * lax.axis_size('shell')), 'shell',...  21 us
    all_to_all x1, starting transfers between devices, per_device(): lax.all_to_all(half_blocks, 'shell', split_axis=1, concat_axis=0, tiled=T...  20.4 us
    all_to_all x1, waiting for transfers between devices, per_device(): lax.all_to_all(lax.all_to_all(half_blocks, 'shell', split_axis=1, concat_...  12.2 us
    all_to_all x1, starting transfers between devices, per_device(): lax.all_to_all(jnp.stack([pair_list] * lax.axis_size('shell')), 'shell',...  8.48 us
    another operation x1, loops' own time, per_device(): half_blocks = lax.map(one_slot, (integrals, pair_list[:, 1]))  7.78 us
    all_to_all x1, starting transfers between devices, per_device(): lax.all_to_all(lax.all_to_all(half_blocks, 'shell', split_axis=1, concat_...  4.18 us
    dot_general x4, matrix products, one_slot(): lax.dot_general(column, int_block.reshape(BS, aux_dev * BS), (((0,), (0,)...  3.97 us
  transfers between devices with their start and end apart: 3, of which 3 were waited for; matrix products, arithmetic and copies ran while one was open for 1% of the time, Pallas kernels for 0%

profile of v1, /device:TPU:1, one launch (start us, length us, event | category | flops | bytes accessed | tf_op | source)
XLA Modules:
  0.0 147.7 jit_solution(13649713370472652099)
XLA Ops:
  0.0 0.7 compare_select_fusion.1
  0.7 1.0 scatter_custom_fusion
  1.7 1.5 %copy.21 = bf16[512,1024]{0,1:T(8,128)(2,1)S(1)} copy(bf16[512,1024]{1,0:T(8,128)(2,1)} %param.9) | data formatting | bytes 2097152 | tf_op args[2]
  3.4 0.2 slice_reduce_fusion
  3.6 0.6 gather_fusion
  4.3 0.2 bitcast_select_fusion
  4.5 14.2 %while.12 = (s32[]{:T(128)}, bf16[4,1024,128]{2,1,0:T(8,128)(2,1)S(1)}, s32[4]{0:T(128)S(1)}, bf16[512,1024]{0,1:T(8,128)(2,1)S(1)}, bf16[4,128,1,128]{3,1,2,0:T...) while((s32[]{:T(128)}, ...), condition=%wide.region_2.3_spmd, body=%wide.region_1.2_spmd.sunk | while | flops 33685520 | bytes 558360 | solution.py:40
  4.5 0.6 dynamic_slice.31
  7.0 1.0 fusion.21
  8.0 0.6 dynamic_slice.31
  10.6 1.0 fusion.21
  11.6 0.6 dynamic_slice.31
  14.1 1.0 fusion.21
  15.1 0.6 dynamic_slice.31
  17.7 1.0 fusion.21
  18.7 1.8 %copy.37 = bf16[4,1024,128]{2,0,1:T(4,128)(2,1)} copy(bf16[4,1024,128]{2,1,0:T(8,128)(2,1)S(1)} %get-tuple-element.71) | data formatting | bytes 2097152 | tf_op jit(solution)/shard_map/while | solution.py:40
  20.5 20.4 %all-to-all-start.1 = ((bf16[4,1024,1,128]{3,0,2,1:T(4,128)(2,1)}), bf16[4,1024,1,128]{3,0,2,1:T(4,128)(2,1)S(1)}, u32[]{:S(2)}, u32[]{:S(2)}) async-start(bf16[4,1024,1,128]{3,0,2,1:T(4,128)(2,1)} %bitcast.41), calls=%async_computation.1 | async-start | bytes 2097152 | tf_op jit(solution)/shard_map/all_to_all | solution.py:50
  41.0 54.3 %all-to-all-done.1 = bf16[4,1024,1,128]{3,0,2,1:T(4,128)(2,1)S(1)} async-done(((bf16[4,1024,1,128]{3,0,2,1:T(4,128)(2,1)}), bf16[4,1024,1,128]{3,0,2,1:T(4,128)(2,1)S(1)}, u32[]{:S(2)}, u32[]{:S(2)}) %all-to-all-start.1) | async-done | bytes 1048608 | tf_op jit(solution)/shard_map/all_to_all | solution.py:50
  95.2 0.7 stack.2
  95.9 8.5 %all-to-all-start = ((s32[128,4,3]{1,2,0:T(4,128)}), s32[128,4,3]{1,2,0:T(4,128)S(1)}, u32[]{:S(2)}, u32[]{:S(2)}) async-start(s32[128,4,3]{1,2,0:T(4,128)} %stack.2), calls=%async_computation | async-start | bytes 524288 | tf_op jit(solution)/shard_map/all_to_all | solution.py:43
  104.4 0.1 copy.36
  104.6 0.2 copy.25
  104.8 1.1 copy.26
  105.9 21.0 %all-to-all-done = s32[128,4,3]{1,2,0:T(4,128)S(1)} async-done(((s32[128,4,3]{1,2,0:T(4,128)}), s32[128,4,3]{1,2,0:T(4,128)S(1)}, u32[]{:S(2)}, u32[]{:S(2)}) %all-to-all-start) | async-done | bytes 6176 | tf_op jit(solution)/shard_map/all_to_all | solution.py:43
  126.9 4.2 %all-to-all-start.2 = ((bf16[512,8,1,128]{3,0,2,1:T(8,128)(2,1)}), bf16[512,8,1,128]{3,0,2,1:T(8,128)(2,1)S(1)}, u32[]{:S(2)}, u32[]{:S(2)}) async-start(bf16[512,8,1,128]{3,0,2,1:T(8,128)(2,1)} %copy.26), calls=%async_computation.2 | async-start | bytes 2097152 | tf_op jit(solution)/shard_map/all_to_all | solution.py:49
  131.1 0.1 reshape.45
  131.3 12.2 %all-to-all-done.2 = bf16[512,8,1,128]{3,0,2,1:T(8,128)(2,1)S(1)} async-done(((bf16[512,8,1,128]{3,0,2,1:T(8,128)(2,1)}), bf16[512,8,1,128]{3,0,2,1:T(8,128)(2,1)S(1)}, u32[]{:S(2)}, u32[]{:S(2)}) %all-to-all-start.2) | async-done | bytes 1048608 | tf_op jit(solution)/shard_map/all_to_all | solution.py:49
  143.6 0.5 copy.27
  144.1 0.8 convolution_convert_fusion.2
  144.8 0.8 reshape.49
  145.6 0.7 fusion.6
  146.3 1.3 copy.35
  (15 shorter events, 0.4 us)
Async XLA Ops:
  0.0 145.6 %copy-start = (bf16[4,4]{1,0:T(4,128)(2,1)S(1)}, bf16[4,4]{1,0:T(4,128)(2,1)}, u32[]{:S(2)}) copy-start(bf16[4,4]{1,0:T(4,128)(2,1)} %param.10) | copy-start | bytes 100
  1.7 1.7 %copy-start.1 = (s32[4,3]{1,0:T(4,128)S(1)}, s32[4,3]{1,0:T(4,128)}, u32[]{:S(2)}) copy-start(s32[4,3]{1,0:T(4,128)} %param.8) | copy-start | bytes 148
  20.5 74.8 %all-to-all-start.1 = ((bf16[4,1024,1,128]{3,0,2,1:T(4,128)(2,1)}), bf16[4,1024,1,128]{3,0,2,1:T(4,128)(2,1)S(1)}, u32[]{:S(2)}, u32[]{:S(2)}) async-start(bf16[4,1024,1,128]{3,0,2,1:T(4,128)(2,1)} %bitcast.41), calls=%async_computation.1 | async-start | bytes 2097152 | tf_op jit(solution)/shard_map/all_to_all | solution.py:50
  95.9 31.0 %all-to-all-start = ((s32[128,4,3]{1,2,0:T(4,128)}), s32[128,4,3]{1,2,0:T(4,128)S(1)}, u32[]{:S(2)}, u32[]{:S(2)}) async-start(s32[128,4,3]{1,2,0:T(4,128)} %stack.2), calls=%async_computation | async-start | bytes 524288 | tf_op jit(solution)/shard_map/all_to_all | solution.py:43
  126.9 16.6 %all-to-all-start.2 = ((bf16[512,8,1,128]{3,0,2,1:T(8,128)(2,1)}), bf16[512,8,1,128]{3,0,2,1:T(8,128)(2,1)S(1)}, u32[]{:S(2)}, u32[]{:S(2)}) async-start(bf16[512,8,1,128]{3,0,2,1:T(8,128)(2,1)} %copy.26), calls=%async_computation.2 | async-start | bytes 2097152 | tf_op jit(solution)/shard_map/all_to_all | solution.py:49
